TPU v7x, 32 devices: a whole 2x2x4 slice. The times are simulated.
32 devices in a mesh: ctx: 8 (over z, core), tp: 4 (over y, x).
Axes of the slice: x: 2, y: 2, z: 4, core: 2. Of those that a mesh axis runs over, the one named last changes fastest.
Arguments:
- tokens: bfloat16 [4096, 4096], P(('ctx', 'tp')), may hold values from -6 to 6
- in_weight: bfloat16 [3, 4096, 2048], P(None, None, 'tp'), may hold values from -0.09375 to 0.09375
- short_taps: float32 [3, 3, 2048], P(None, None, 'tp'), may hold values from -3 to 3
- decay_rate: float32 [16, 2048], P(None, 'tp'), may hold values from 4.8828125e-05 to 0.0333333333
- residue: float32 [16, 2048], P(None, 'tp'), may hold values from -0.26 to 0.26
- skip_gain: float32 [2048], P('tp'), may hold values from -4 to 4
- grad_out: bfloat16 [4096, 2048], P('ctx', 'tp'), may hold values from -6 to 6
Outputs:
- mixed_out: bfloat16 [4096, 2048], P('ctx', 'tp')
- input_grad: bfloat16 [4096, 4096], P(('ctx', 'tp'))
All inputs are finite; a program needn't handle non-finite values.
Results may differ from a plain program's by a relative error of at most 0.0065.
Values may be sent and summed in bfloat16 or wider, within the bound.
A program may use at most 192 MiB of HBM per device.

v0:
```python
import functools

import jax
import jax.numpy as jnp
from jax import lax
from jax.experimental import pallas as pl
from jax.experimental.pallas import tpu as pltpu
from jax.sharding import PartitionSpec as P

exact_mode = lax.Precision.HIGHEST


def from_behind(value, axis, steps):
    count = lax.axis_size(axis)
    leading, last = (max(0, -steps), min(count, count - steps))
    return lax.ppermute(value, axis, [(source, source + steps) for source in range(leading, last)])


def modal_block(signal, log_pole, residue):
    length, channels = signal.shape
    sub_len = min(64, length)
    sub_count = length // sub_len
    offsets = jnp.arange(sub_len, dtype=jnp.float32)
    sections = signal.reshape(sub_count, sub_len, channels)
    powers = jnp.exp(log_pole[:, None, :] * offsets[None, :, None])
    filter_taps = jnp.sum(residue[:, None, :] * powers, axis=0)
    lag_index = jnp.arange(sub_len)[:, None] - jnp.arange(sub_len)[None, :]
    toeplitz = jnp.where((lag_index >= 0)[:, :, None], filter_taps[jnp.maximum(lag_index, 0)], 0.0)
    within = jnp.einsum("abc,kbc->kac", toeplitz, sections, precision=exact_mode)
    to_end = jnp.exp(log_pole[:, None, :] * (sub_len - 1.0 - offsets)[None, :, None])
    end_states = jnp.einsum("nbc,kbc->nkc", to_end, sections, precision=exact_mode)
    lag_blocks = jnp.arange(sub_count + 1)[:, None] - 1 - jnp.arange(sub_count)[None, :]
    valid_lag = lag_blocks >= 0
    lag_float = (jnp.maximum(lag_blocks, 0) * sub_len).astype(jnp.float32)
    decay_table = jnp.exp(log_pole[None, None] * lag_float[:, :, None, None])
    decay_table = jnp.where(valid_lag[:, :, None, None], decay_table, 0.0)
    carried = jnp.einsum("kmnc,nmc->nkc", decay_table, end_states, precision=exact_mode)
    stepped = residue[:, None, :] * jnp.exp(log_pole[:, None, :] * (offsets[None, :, None] + 1.0))
    output = within + jnp.einsum(
        "nac,nkc->kac", stepped, carried[:, :sub_count], precision=exact_mode
    )
    return (output.reshape(length, channels), carried[:, sub_count])


def carry_term(incoming, log_pole, residue, length):
    channels = incoming.shape[1]
    sub_len = min(64, length)
    sub_count = length // sub_len
    offsets = jnp.arange(sub_len, dtype=jnp.float32)
    stepped = residue[:, None, :] * jnp.exp(log_pole[:, None, :] * (offsets[None, :, None] + 1.0))
    block_starts = (jnp.arange(sub_count) * sub_len).astype(jnp.float32)
    start_states = incoming[:, None, :] * jnp.exp(
        log_pole[:, None, :] * block_starts[None, :, None]
    )
    output = jnp.einsum("nac,nkc->kac", stepped, start_states, precision=exact_mode)
    return output.reshape(length, channels)


def shards(tokens, in_weight, short_taps, decay_rate, residue, skip_gain, grad_out):
    width = in_weight.shape[2]
    weight_cat = jnp.concatenate([in_weight[0], in_weight[1], in_weight[2]], axis=1)
    streams = jnp.dot(
        lax.all_gather(tokens, "tp", axis=0, tiled=True),
        weight_cat,
        preferred_element_type=jnp.float32,
    ).astype(jnp.bfloat16)
    length = streams.shape[0]
    tap_reach = short_taps.shape[1] - 1
    taps_cat = jnp.concatenate([short_taps[0], short_taps[1], short_taps[2]], axis=1)
    before = from_behind(streams[length - tap_reach :], "ctx", 1)
    extended = jnp.concatenate([before, streams], axis=0).astype(jnp.float32)
    short_mixed = taps_cat[0][None] * extended[tap_reach:]
    for offset in range(1, tap_reach + 1):
        short_mixed = (
            short_mixed
            + taps_cat[offset][None] * extended[tap_reach - offset : tap_reach - offset + length]
        )
    query_side = short_mixed[:, :width]
    key_side = short_mixed[:, width : 2 * width]
    value_side = short_mixed[:, 2 * width :]
    product_in = key_side * value_side
    log_pole = -decay_rate
    forward_local, forward_sum = modal_block(product_in, log_pole, residue)
    upstream = grad_out.astype(jnp.float32)
    conv_grad = upstream * query_side
    backward_local, backward_sum = modal_block(conv_grad[::-1], log_pole, residue)
    position = lax.axis_index("ctx")
    summaries = (
        lax.all_gather(forward_sum[None], "ctx", axis=0, tiled=True),
        lax.all_gather(backward_sum[None], "ctx", axis=0, tiled=True),
    )
    block_index = jnp.arange(summaries[0].shape[0])
    earlier_gap = position - 1 - block_index
    later_gap = block_index - position - 1
    scale_fwd = (jnp.maximum(earlier_gap, 0) * length).astype(jnp.float32)
    scale_bwd = (jnp.maximum(later_gap, 0) * length).astype(jnp.float32)
    weight_fwd = jnp.where(
        (earlier_gap >= 0)[:, None, None], jnp.exp(log_pole[None] * scale_fwd[:, None, None]), 0.0
    )
    weight_bwd = jnp.where(
        (later_gap >= 0)[:, None, None], jnp.exp(log_pole[None] * scale_bwd[:, None, None]), 0.0
    )
    incoming_fwd = jnp.sum(weight_fwd * summaries[0], axis=0)
    incoming_bwd = jnp.sum(weight_bwd * summaries[1], axis=0)
    conv_out = forward_local + carry_term(incoming_fwd, log_pole, residue, length)
    back_conv = (backward_local + carry_term(incoming_bwd, log_pole, residue, length))[::-1]
    filtered = conv_out + skip_gain[None] * product_in
    result = (query_side * filtered).astype(jnp.bfloat16)
    grad_query = upstream * filtered
    grad_product = back_conv + skip_gain[None] * conv_grad
    stream_grads = jnp.concatenate(
        [grad_query, grad_product * value_side, grad_product * key_side], axis=1
    )
    after_rows = from_behind(stream_grads[:tap_reach], "ctx", -1)
    padded = jnp.concatenate([stream_grads, after_rows], axis=0)
    grad_streams = taps_cat[0][None] * padded[:length]
    for offset in range(1, tap_reach + 1):
        grad_streams = grad_streams + taps_cat[offset][None] * padded[offset : offset + length]
    grad_streams = grad_streams.astype(jnp.bfloat16)
    input_grad = lax.psum_scatter(
        jnp.einsum("rk,dk->rd", grad_streams, weight_cat, preferred_element_type=jnp.float32),
        "tp",
        scatter_dimension=0,
        tiled=True,
    )
    return (result, input_grad.astype(jnp.bfloat16))


MESH = pl.DeviceIdType.MESH
SUBLANES = 8
LANES = 128
ROWS = 32
VMEM_LIMIT = 60 * 1024 * 1024


def vmem_specs(count):
    return [pl.BlockSpec(memory_space=pltpu.VMEM)] * count


def square_partners():
    me = lax.axis_index("tp")
    y, x = me // 2, me % 2
    return me, y * 2 + (1 - x), (1 - y) * 2 + x, (1 - y) * 2 + (1 - x)


def announce(axis, partners):
    barrier = pltpu.get_barrier_semaphore()
    for partner in partners:
        pl.semaphore_signal(barrier, inc=1, device_id={axis: partner}, device_id_type=MESH)
    return lambda: pl.semaphore_wait(barrier, len(partners))


def greet(axis, partners):
    announce(axis, partners)()


def project_kernel(tok_ref, w_hbm, out_ref, held, w_buf, w_sem, send_sem, recv_sem):
    rows = tok_ref.shape[0]
    half, part_rows = rows // 2, rows // 4
    width = w_hbm.shape[2]
    tile = w_buf.shape[2]
    per_stream = width // tile
    me, xn, yn, dg = square_partners()
    loads = []
    for part in range(3 * per_stream):
        stream, col = divmod(part, per_stream)
        load = pltpu.make_async_copy(
            w_hbm.at[stream, :, pl.ds(col * tile, tile)], w_buf.at[part], w_sem.at[part]
        )
        load.start()
        loads.append(load)
    greet("tp", (xn, yn))

    def send(index, source, slot, start, partner):
        return pltpu.make_async_remote_copy(
            src_ref=source,
            dst_ref=held.at[slot, pl.ds(start, source.shape[0])],
            send_sem=send_sem.at[index],
            recv_sem=recv_sem.at[index],
            device_id={"tp": partner},
            device_id_type=MESH,
        )

    own_a, own_b = tok_ref.at[pl.ds(0, half)], tok_ref.at[pl.ds(half, half)]
    copies = [
        send(0, own_a, 0, 0, xn),
        send(1, own_b, 1, half, yn),
        send(2, own_b, 0, half, xn),
        send(3, own_a, 1, 0, yn),
        send(4, held.at[0, pl.ds(0, part_rows)], 2, 0, yn),
        send(5, held.at[1, pl.ds(half, part_rows)], 2, part_rows, xn),
        send(6, held.at[0, pl.ds(part_rows, part_rows)], 2, half, yn),
        send(7, held.at[1, pl.ds(half + part_rows, part_rows)], 2, half + part_rows, xn),
    ]
    for index in range(4):
        copies[index].start()

    def multiply(block, owner):
        start = pl.multiple_of(owner * rows, rows)

        @pl.loop(0, 3 * per_stream)
        def _(part):
            out_ref[part, pl.ds(start, rows), :] = jnp.dot(
                block[...], w_buf[part], preferred_element_type=jnp.float32
            ).astype(out_ref.dtype)

    for load in loads:
        load.wait()
    multiply(tok_ref, me)
    copies[0].wait_recv()
    copies[4].start()
    copies[6].start()
    copies[1].wait_recv()
    copies[5].start()
    copies[7].start()
    copies[2].wait_recv()
    multiply(held.at[0], xn)
    copies[3].wait_recv()
    multiply(held.at[1], yn)
    for step in range(2):
        copies[4 + 2 * step].wait_recv()
        copies[5 + 2 * step].wait_recv()
        upper = pl.multiple_of(dg * rows + step * part_rows, part_rows)
        lower = pl.multiple_of(dg * rows + half + step * part_rows, part_rows)
        block = held.at[2, pl.ds(step * half, half)]

        @pl.loop(0, 3 * per_stream)
        def _(part, block=block, upper=upper, lower=lower):
            value = jnp.dot(
                block[...], w_buf[part], preferred_element_type=jnp.float32
            ).astype(out_ref.dtype)
            out_ref[part, pl.ds(upper, part_rows), :] = value[:part_rows]
            out_ref[part, pl.ds(lower, part_rows), :] = value[part_rows:]

    for copy in copies:
        copy.wait_send()


def gather_project(tokens, in_weight):
    rows, depth = tokens.shape
    streams, _, width = in_weight.shape
    tile = min(256, width)
    parts = streams * (width // tile)
    return pl.pallas_call(
        project_kernel,
        out_shape=jax.ShapeDtypeStruct((parts, 4 * rows, tile), jnp.bfloat16),
        in_specs=[pl.BlockSpec(memory_space=pltpu.VMEM), pl.BlockSpec(memory_space=pl.ANY)],
        out_specs=pl.BlockSpec(memory_space=pltpu.VMEM),
        scratch_shapes=[
            pltpu.VMEM((3, rows, depth), jnp.bfloat16),
            pltpu.VMEM((parts, depth, tile), jnp.bfloat16),
            pltpu.SemaphoreType.DMA((parts,)),
            pltpu.SemaphoreType.DMA((8,)),
            pltpu.SemaphoreType.DMA((8,)),
        ],
        compiler_params=pltpu.CompilerParams(
            collective_id=0, has_side_effects=True, vmem_limit_bytes=VMEM_LIMIT
        ),
    )(tokens, in_weight)


def tree_sum(values):
    while len(values) > 1:
        values = [a + b for a, b in zip(values[::2], values[1::2])] + (
            [values[-1]] if len(values) % 2 else []
        )
    return values[0]


def middle_kernel(
    count, st_ref, taps_ref, rate_ref, res_ref, skip_ref, grad_ref, mixed_ref, gs_ref,
    ext, side, prod, cgrad, conv, back, sgrad, halo, pole, carry_f, carry_b,
    mine_f, mine_b, all_f, all_b, inc_f, inc_b,
    send_f, recv_f, send_b, recv_b, send_h, recv_h,
):
    parts, length, tile = st_ref.shape
    width = mixed_ref.shape[1]
    per_stream = width // tile
    modes = rate_ref.shape[0]
    section = length // SUBLANES
    chunks = length // ROWS
    me = lax.axis_index("ctx")
    after, prior = lax.rem(me + 1, count), lax.rem(me + count - 1, count)
    entered = announce("ctx", [lax.rem(me + step, count) for step in range(1, count)])

    def neighbour(index, source, target, partner):
        return pltpu.make_async_remote_copy(
            src_ref=source,
            dst_ref=target,
            send_sem=send_h.at[index],
            recv_sem=recv_h.at[index],
            device_id={"ctx": partner},
            device_id_type=MESH,
        )

    first = neighbour(0, st_ref.at[:, pl.ds(length - 16, 16), :], halo, after)
    pole[...] = jnp.exp(-rate_ref[...])

    @pl.loop(0, chunks)
    def _(step):
        start = pl.multiple_of(step * ROWS, ROWS)
        for part in range(parts):
            ext[pl.ds(start + 8, ROWS), part * tile : (part + 1) * tile] = st_ref[
                part, pl.ds(start, ROWS), :
            ].astype(jnp.float32)

    entered()
    first.start()

    def short_mix(start):
        for col in range(0, width, LANES):
            lanes = slice(col, col + LANES)
            mixed = []
            for s in range(3):
                block = ext[pl.ds(start, ROWS + 8), s * width + col : s * width + col + LANES]
                value = taps_ref[s, 0:1, lanes] * block[8:]
                for j in range(1, 3):
                    value = value + taps_ref[s, j : j + 1, lanes] * block[8 - j : 8 - j + ROWS]
                side[s, pl.ds(start, ROWS), lanes] = value
                mixed.append(value)
            prod[col // LANES, pl.ds(start, ROWS), :] = mixed[1] * mixed[2]
            cgrad[col // LANES, pl.ds(start, ROWS), :] = (
                grad_ref[pl.ds(start, ROWS), lanes].astype(jnp.float32) * mixed[0]
            )

    @pl.loop(1, chunks)
    def _(step):
        short_mix(pl.multiple_of(step * ROWS, ROWS))

    first.wait_recv()
    keep = jnp.where(me > 0, 1.0, 0.0).astype(jnp.float32)
    for part in range(parts):
        ext[0:8, part * tile : (part + 1) * tile] = (
            halo[part].astype(jnp.float32)[8:16] * keep
        )

    short_mix(0)

    tiles = width // LANES
    sub = lax.broadcasted_iota(jnp.int32, (SUBLANES, LANES), 0)

    def wide(ref, lanes):
        return [
            jnp.broadcast_to(ref[n : n + 1, lanes], (SUBLANES, LANES)) for n in range(modes)
        ]

    def end_states(source, carry, mine, reverse):
        @pl.loop(0, tiles)
        def _(t):
            lanes = pl.ds(pl.multiple_of(t * LANES, LANES), LANES)
            p = wide(pole, lanes)

            def body(i, state):
                j = section - 1 - i if reverse else i
                x = source[t, pl.ds(j, SUBLANES, stride=section), :]
                return [a * b + x for a, b in zip(p, state)]

            zero = jnp.zeros((SUBLANES, LANES), jnp.float32)
            ends = lax.fori_loop(0, section, body, [zero] * modes, unroll=4)
            for n in range(modes):
                rate = rate_ref[n : n + 1, lanes]
                total = ends[n] * res_ref[n : n + 1, lanes]
                for k in (1, 2, 4):
                    decay = jnp.exp(rate * (-1.0 * section * k))
                    moved = pltpu.roll(total, SUBLANES - k if reverse else k, 0)
                    inside = sub < SUBLANES - k if reverse else sub >= k
                    total = total + jnp.where(inside, decay * moved, 0.0)
                moved = pltpu.roll(total, SUBLANES - 1 if reverse else 1, 0)
                inside = sub < SUBLANES - 1 if reverse else sub >= 1
                carry[n, :, lanes] = jnp.where(inside, moved, 0.0)
                mine[n : n + 1, lanes] = total[0:1] if reverse else total[SUBLANES - 1 :]

    def incoming_at(incoming, lanes, reverse):
        steps = (SUBLANES - 1 - sub if reverse else sub).astype(jnp.float32) * (-1.0 * section)
        return [
            jnp.exp(rate_ref[n : n + 1, lanes] * steps) * incoming[n : n + 1, lanes]
            for n in range(modes)
        ]

    def local_scan(source, target, carry, incoming, reverse):
        @pl.loop(0, tiles)
        def _(t):
            lanes = pl.ds(pl.multiple_of(t * LANES, LANES), LANES)
            p, r = wide(pole, lanes), wide(res_ref, lanes)

            def body(i, state):
                j = section - 1 - i if reverse else i
                x = source[t, pl.ds(j, SUBLANES, stride=section), :]
                state = [a * b + c * x for a, b, c in zip(p, state, r)]
                target[t, pl.ds(j, SUBLANES, stride=section), :] = tree_sum(state)
                return state

            start = [carry[n, :, lanes] for n in range(modes)]
            if incoming is not None:
                arrived = incoming_at(incoming, lanes, reverse)
                start = [a + b for a, b in zip(start, arrived)]
            lax.fori_loop(0, section, body, start, unroll=2)

    def summary(mine, table, send_sem, recv_sem, source, partner):
        return pltpu.make_async_remote_copy(
            src_ref=mine,
            dst_ref=table.at[source],
            send_sem=send_sem.at[partner],
            recv_sem=recv_sem.at[source],
            device_id={"ctx": partner},
            device_id_type=MESH,
        )

    forward = functools.partial(summary, mine_f, all_f, send_f, recv_f)
    backward = functools.partial(summary, mine_b, all_b, send_b, recv_b)

    end_states(cgrad, carry_b, mine_b, True)
    for other in range(count):

        @pl.when(other < me)
        def _(other=other):
            backward(me, other).start()

    end_states(prod, carry_f, mine_f, False)
    for other in range(count):

        @pl.when(other > me)
        def _(other=other):
            forward(me, other).start()

    local_scan(prod, conv, carry_f, None, False)

    def add_carry(target, incoming, reverse):
        @pl.loop(0, tiles)
        def _(t):
            lanes = pl.ds(pl.multiple_of(t * LANES, LANES), LANES)
            p = wide(pole, lanes)
            state = incoming_at(incoming, lanes, reverse)

            def body(i, state):
                j = section - 1 - i if reverse else i
                state = [a * b for a, b in zip(p, state)]
                place = pl.ds(j, SUBLANES, stride=section)
                target[t, place, :] = target[t, place, :] + tree_sum(state)
                return state

            lax.fori_loop(0, section, body, state, unroll=2)

    inc_b[...] = jnp.zeros_like(inc_b)
    for other in range(count):

        @pl.when(other > me)
        def _(other=other):
            backward(other, me).wait_recv()
            gap = ((me + 1 - other) * length).astype(jnp.float32)
            inc_b[...] += jnp.exp(rate_ref[...] * gap) * all_b[other]

    local_scan(cgrad, back, carry_b, inc_b, True)
    inc_f[...] = jnp.zeros_like(inc_f)
    for other in range(count):

        @pl.when(other < me)
        def _(other=other):
            forward(other, me).wait_recv()
            gap = ((other + 1 - me) * length).astype(jnp.float32)
            inc_f[...] += jnp.exp(rate_ref[...] * gap) * all_f[other]

    add_carry(conv, inc_f, False)


    def finish(start):
        for col in range(0, width, LANES):
            lanes = slice(col, col + LANES)
            rows = pl.ds(start, ROWS)
            skip = skip_ref[0:1, lanes]
            filtered = conv[col // LANES, rows, :] + skip * prod[col // LANES, rows, :]
            mixed_ref[rows, lanes] = (side[0, rows, lanes] * filtered).astype(mixed_ref.dtype)
            product = back[col // LANES, rows, :] + skip * cgrad[col // LANES, rows, :]
            upstream = grad_ref[rows, lanes].astype(jnp.float32)
            sgrad[rows, lanes] = upstream * filtered
            sgrad[rows, width + col : width + col + LANES] = product * side[2, rows, lanes]
            sgrad[rows, 2 * width + col : 2 * width + col + LANES] = product * side[1, rows, lanes]

    finish(0)
    last = neighbour(1, sgrad.at[pl.ds(0, 8)], sgrad.at[pl.ds(length, 8)], prior)
    last.start()

    @pl.loop(1, chunks)
    def _(step):
        finish(pl.multiple_of(step * ROWS, ROWS))

    def transpose_taps(start):
        for s in range(3):
            for col in range(0, width, LANES):
                lanes = slice(s * width + col, s * width + col + LANES)
                block = sgrad[pl.ds(start, ROWS + 8), lanes]
                value = taps_ref[s, 0:1, col : col + LANES] * block[:ROWS]
                for j in range(1, 3):
                    value = value + taps_ref[s, j : j + 1, col : col + LANES] * block[j : j + ROWS]
                gs_ref[pl.ds(start, ROWS), lanes] = value.astype(gs_ref.dtype)

    @pl.loop(0, chunks - 1)
    def _(step):
        transpose_taps(pl.multiple_of(step * ROWS, ROWS))

    last.wait_recv()

    @pl.when(me == count - 1)
    def _():
        sgrad[length : length + 8, :] = jnp.zeros((8, 3 * width), jnp.float32)

    transpose_taps(length - ROWS)
    first.wait_send()
    last.wait_send()
    for other in range(count):

        @pl.when(other > me)
        def _(other=other):
            forward(me, other).wait_send()

        @pl.when(other < me)
        def _(other=other):
            backward(me, other).wait_send()


def middle(streams, short_taps, decay_rate, residue, skip_gain, grad_out):
    count = lax.axis_size("ctx")
    parts, length, tile = streams.shape
    modes, width = decay_rate.shape
    f32 = jnp.float32
    table = pltpu.VMEM((modes, width), f32)
    tables = pltpu.VMEM((count, modes, width), f32)
    plane = pltpu.VMEM((width // LANES, length, LANES), f32)
    carry = pltpu.VMEM((modes, SUBLANES, width), f32)
    dma = pltpu.SemaphoreType.DMA
    return pl.pallas_call(
        functools.partial(middle_kernel, count),
        out_shape=(
            jax.ShapeDtypeStruct((length, width), jnp.bfloat16),
            jax.ShapeDtypeStruct((length, 3 * width), jnp.bfloat16),
        ),
        in_specs=vmem_specs(6),
        out_specs=tuple(vmem_specs(2)),
        scratch_shapes=[
            pltpu.VMEM((length + 8, 3 * width), f32),
            pltpu.VMEM((3, length, width), f32),
            plane, plane, plane, plane,
            pltpu.VMEM((length + 8, 3 * width), f32),
            pltpu.VMEM((parts, 16, tile), jnp.bfloat16),
            table, carry, carry, table, table, tables, tables, table, table,
            dma((count,)), dma((count,)), dma((count,)), dma((count,)), dma((2,)), dma((2,)),
        ],
        compiler_params=pltpu.CompilerParams(
            collective_id=1, has_side_effects=True, vmem_limit_bytes=VMEM_LIMIT
        ),
    )(streams, short_taps, decay_rate, residue, skip_gain[None], grad_out)


def scatter_kernel(gs_ref, w_hbm, out_ref, w_buf, out_buf, in_buf, own, w_sem, send_sem, recv_sem):
    rows, depth = out_ref.shape
    pieces, streams, cols, width = w_buf.shape
    half = pieces // 2
    me, xn, yn, dg = square_partners()

    def load(piece):
        return pltpu.make_async_copy(
            w_hbm.at[:, pl.ds(piece * cols, cols), :], w_buf.at[piece], w_sem.at[piece]
        )

    for piece in range(half):
        load(piece).start()
        load(half + piece).start()
    entered = announce("tp", (xn, yn))

    def send(kind, piece, partner):
        return pltpu.make_async_remote_copy(
            src_ref=out_buf.at[kind, piece],
            dst_ref=in_buf.at[kind, piece],
            send_sem=send_sem.at[kind, piece],
            recv_sem=recv_sem.at[kind, piece],
            device_id={"tp": partner},
            device_id_type=MESH,
        )

    def partial(owner, piece):
        block = pl.ds(pl.multiple_of(owner * rows, rows), rows)
        total = None
        for s in range(streams):
            term = lax.dot_general(
                gs_ref[block, s * width : (s + 1) * width],
                w_buf[piece, s],
                (((1,), (1,)), ((), ())),
                preferred_element_type=jnp.float32,
            )
            total = term if total is None else total + term
        return total

    def emit(kind, piece, value, partner):
        out_buf[kind, piece] = value.astype(out_buf.dtype)
        send(kind, piece, partner).start()

    load(0).wait()
    opening = partial(dg, 0)
    entered()
    emit(0, 0, opening, xn)
    load(half).wait()
    emit(0, half, partial(dg, half), yn)

    @pl.loop(1, half)
    def _(k):
        load(k).wait()
        emit(0, k, partial(dg, k), xn)
        load(half + k).wait()
        emit(0, half + k, partial(dg, half + k), yn)

    @pl.loop(0, half)
    def _(k):
        emit(1, k, partial(xn, k), xn)
        emit(2, half + k, partial(yn, half + k), yn)

    @pl.loop(0, half)
    def _(k):
        own_x, own_y = partial(xn, half + k), partial(yn, k)
        send(0, half + k, yn).wait_recv()
        emit(1, half + k, own_x + in_buf[0, half + k].astype(jnp.float32), xn)
        send(0, k, xn).wait_recv()
        emit(2, k, own_y + in_buf[0, k].astype(jnp.float32), yn)

    @pl.loop(0, pieces)
    def _(k):
        own[k] = partial(me, k)

    for k in [k + offset for k in range(half) for offset in (0, half)]:
        send(1, k, xn).wait_recv()
        send(2, k, yn).wait_recv()
        out_ref[:, k * cols : (k + 1) * cols] = (
            own[k] + in_buf[1, k].astype(jnp.float32) + in_buf[2, k].astype(jnp.float32)
        ).astype(out_ref.dtype)
    for k in range(pieces):
        send(0, k, xn if k < half else yn).wait_send()
        send(1, k, xn).wait_send()
        send(2, k, yn).wait_send()


def project_back(grad_streams, in_weight):
    length = grad_streams.shape[0]
    streams, depth, width = in_weight.shape
    rows, pieces = length // 4, 8
    cols = depth // pieces
    travelling = pltpu.VMEM((3, pieces, rows, cols), jnp.bfloat16)
    return pl.pallas_call(
        scatter_kernel,
        out_shape=jax.ShapeDtypeStruct((rows, depth), jnp.bfloat16),
        in_specs=[pl.BlockSpec(memory_space=pltpu.VMEM), pl.BlockSpec(memory_space=pl.ANY)],
        out_specs=pl.BlockSpec(memory_space=pltpu.VMEM),
        scratch_shapes=[
            pltpu.VMEM((pieces, streams, cols, width), jnp.bfloat16),
            travelling,
            travelling,
            pltpu.VMEM((pieces, rows, cols), jnp.float32),
            pltpu.SemaphoreType.DMA((pieces,)),
            pltpu.SemaphoreType.DMA((3, pieces)),
            pltpu.SemaphoreType.DMA((3, pieces)),
        ],
        compiler_params=pltpu.CompilerParams(
            collective_id=2, has_side_effects=True, vmem_limit_bytes=VMEM_LIMIT
        ),
    )(grad_streams, in_weight)


def square_shards(tokens, in_weight, short_taps, decay_rate, residue, skip_gain, grad_out):
    streams = gather_project(tokens, in_weight)
    mixed_out, grad_streams = middle(
        streams, short_taps, decay_rate, residue, skip_gain, grad_out
    )
    return mixed_out, project_back(grad_streams, in_weight)


def solution(mesh):
    in_specs = (
        P(("ctx", "tp"), None),
        P(None, None, "tp"),
        P(None, None, "tp"),
        P(None, "tp"),
        P(None, "tp"),
        P("tp"),
        P("ctx", "tp"),
    )
    out_specs = (P("ctx", "tp"), P(("ctx", "tp"), None))
    body = square_shards if mesh.shape["tp"] == 4 else shards
    return jax.shard_map(body, mesh=mesh, in_specs=in_specs, out_specs=out_specs, check_vma=False)
```

profile of v0, /device:TPU:0, one launch (start us, length us, event | category | flops | bytes accessed | tf_op | source)
XLA Modules:
  0.0 113.5 jit_solution(10686981716389543108)
XLA Ops:
  0.6 44.1 %shard_map.86.st_ref = bf16[6,512,256]{2,1,0:T(8,128)(2,1)} custom-call(bf16[128,4096]{1,0:T(8,128)(2,1)} %tok_ref.1, bf16[3,4096,512]{2,1,0:T(8,128)(2,1)} %w_hbm.3), custom_call_target="tpu_custom_call" | custom-call | tf_op jit(solution)/shard_map/pallas_call | solution.py:244
  44.8 25.8 %shard_map.87 = (bf16[512,512]{1,0:T(8,128)(2,1)}, bf16[512,1536]{1,0:T(8,128)(2,1)}) custom-call(bf16[6,512,256]{2,1,0:T(8,128)(2,1)} %shard_map.86.st_ref, f32[3,3,512]{2,1,0:T(4,128)} %taps_ref.1, f32[16,512]{1,0:T(8,128)} %rate_ref.1, f32[16,512]{1,0:T(8,128)} %res_ref.1, f32[1,512]{1,0:T(1,128)} %bitcast.1, bf16[512,512]{1,0:T(8,128)(2,1)} %grad_ref.1), custom_call_target="tpu_custom_call" | custom-call | tf_op jit(solution)/shard_map/pallas_call | solution.py:531
  70.6 0.0 copy-start.1
  70.6 40.4 %shard_map.88 = bf16[128,4096]{1,0:T(8,128)(2,1)} custom-call(bf16[512,1536]{1,0:T(8,128)(2,1)} %get-tuple-element.5.gs_ref, bf16[3,4096,512]{2,1,0:T(8,128)(2,1)} %w_hbm.3), custom_call_target="tpu_custom_call" | custom-call | tf_op jit(solution)/shard_map/pallas_call | solution.py:646
  111.1 0.0 copy-done.1
  111.1 0.0 copy-start
  111.1 0.8 copy.11
  111.9 0.6 copy-done
  112.5 1.0 copy.12
Async XLA Ops:
  70.6 40.5 %copy-start.1 = (bf16[512,512]{1,0:T(8,128)(2,1)S(1)}, bf16[512,512]{1,0:T(8,128)(2,1)}, u32[]{:S(2)}) copy-start(bf16[512,512]{1,0:T(8,128)(2,1)} %get-tuple-element.8) | copy-start | bytes 1572868
  111.1 1.4 %copy-start = (bf16[128,4096]{1,0:T(8,128)(2,1)S(1)}, bf16[128,4096]{1,0:T(8,128)(2,1)}, u32[]{:S(2)}) copy-start(bf16[128,4096]{1,0:T(8,128)(2,1)} %shard_map.88) | copy-start | bytes 3145732
where the time goes:
time: 114 us; the launch traced here: 113 us
  Pallas kernels  110 us (96%)
  local copies, waits for them, and re-layouts  2.38 us (2%)
    pallas_call x1, Pallas kernels, gather_project(): pl.pallas_call(project_kernel, out_shape=jax.ShapeDtypeStruct((parts, 4 *...  44.1 us
    pallas_call x1, Pallas kernels, project_back(): pl.pallas_call(scatter_kernel, out_shape=jax.ShapeDtypeStruct((rows, dept...  40.4 us
    pallas_call x1, Pallas kernels, middle(): pl.pallas_call(functools.partial(middle_kernel, count), out_shape=(jax.Sh...  25.8 us
    unnamed x6, local copies, waits for them, and re-layouts  2.38 us

commit v1 on v0

v1 whole, which is shorter than its diff:
```python
import functools

import jax
import jax.numpy as jnp
from jax import lax
from jax.experimental import pallas as pl
from jax.experimental.pallas import tpu as pltpu
from jax.sharding import PartitionSpec as P

exact_mode = lax.Precision.HIGHEST


def from_behind(value, axis, steps):
    count = lax.axis_size(axis)
    leading, last = (max(0, -steps), min(count, count - steps))
    return lax.ppermute(value, axis, [(source, source + steps) for source in range(leading, last)])


def modal_block(signal, log_pole, residue):
    length, channels = signal.shape
    sub_len = min(64, length)
    sub_count = length // sub_len
    offsets = jnp.arange(sub_len, dtype=jnp.float32)
    sections = signal.reshape(sub_count, sub_len, channels)
    powers = jnp.exp(log_pole[:, None, :] * offsets[None, :, None])
    filter_taps = jnp.sum(residue[:, None, :] * powers, axis=0)
    lag_index = jnp.arange(sub_len)[:, None] - jnp.arange(sub_len)[None, :]
    toeplitz = jnp.where((lag_index >= 0)[:, :, None], filter_taps[jnp.maximum(lag_index, 0)], 0.0)
    within = jnp.einsum("abc,kbc->kac", toeplitz, sections, precision=exact_mode)
    to_end = jnp.exp(log_pole[:, None, :] * (sub_len - 1.0 - offsets)[None, :, None])
    end_states = jnp.einsum("nbc,kbc->nkc", to_end, sections, precision=exact_mode)
    lag_blocks = jnp.arange(sub_count + 1)[:, None] - 1 - jnp.arange(sub_count)[None, :]
    valid_lag = lag_blocks >= 0
    lag_float = (jnp.maximum(lag_blocks, 0) * sub_len).astype(jnp.float32)
    decay_table = jnp.exp(log_pole[None, None] * lag_float[:, :, None, None])
    decay_table = jnp.where(valid_lag[:, :, None, None], decay_table, 0.0)
    carried = jnp.einsum("kmnc,nmc->nkc", decay_table, end_states, precision=exact_mode)
    stepped = residue[:, None, :] * jnp.exp(log_pole[:, None, :] * (offsets[None, :, None] + 1.0))
    output = within + jnp.einsum(
        "nac,nkc->kac", stepped, carried[:, :sub_count], precision=exact_mode
    )
    return (output.reshape(length, channels), carried[:, sub_count])


def carry_term(incoming, log_pole, residue, length):
    channels = incoming.shape[1]
    sub_len = min(64, length)
    sub_count = length // sub_len
    offsets = jnp.arange(sub_len, dtype=jnp.float32)
    stepped = residue[:, None, :] * jnp.exp(log_pole[:, None, :] * (offsets[None, :, None] + 1.0))
    block_starts = (jnp.arange(sub_count) * sub_len).astype(jnp.float32)
    start_states = incoming[:, None, :] * jnp.exp(
        log_pole[:, None, :] * block_starts[None, :, None]
    )
    output = jnp.einsum("nac,nkc->kac", stepped, start_states, precision=exact_mode)
    return output.reshape(length, channels)


def shards(tokens, in_weight, short_taps, decay_rate, residue, skip_gain, grad_out):
    width = in_weight.shape[2]
    weight_cat = jnp.concatenate([in_weight[0], in_weight[1], in_weight[2]], axis=1)
    streams = jnp.dot(
        lax.all_gather(tokens, "tp", axis=0, tiled=True),
        weight_cat,
        preferred_element_type=jnp.float32,
    ).astype(jnp.bfloat16)
    length = streams.shape[0]
    tap_reach = short_taps.shape[1] - 1
    taps_cat = jnp.concatenate([short_taps[0], short_taps[1], short_taps[2]], axis=1)
    before = from_behind(streams[length - tap_reach :], "ctx", 1)
    extended = jnp.concatenate([before, streams], axis=0).astype(jnp.float32)
    short_mixed = taps_cat[0][None] * extended[tap_reach:]
    for offset in range(1, tap_reach + 1):
        short_mixed = (
            short_mixed
            + taps_cat[offset][None] * extended[tap_reach - offset : tap_reach - offset + length]
        )
    query_side = short_mixed[:, :width]
    key_side = short_mixed[:, width : 2 * width]
    value_side = short_mixed[:, 2 * width :]
    product_in = key_side * value_side
    log_pole = -decay_rate
    forward_local, forward_sum = modal_block(product_in, log_pole, residue)
    upstream = grad_out.astype(jnp.float32)
    conv_grad = upstream * query_side
    backward_local, backward_sum = modal_block(conv_grad[::-1], log_pole, residue)
    position = lax.axis_index("ctx")
    summaries = (
        lax.all_gather(forward_sum[None], "ctx", axis=0, tiled=True),
        lax.all_gather(backward_sum[None], "ctx", axis=0, tiled=True),
    )
    block_index = jnp.arange(summaries[0].shape[0])
    earlier_gap = position - 1 - block_index
    later_gap = block_index - position - 1
    scale_fwd = (jnp.maximum(earlier_gap, 0) * length).astype(jnp.float32)
    scale_bwd = (jnp.maximum(later_gap, 0) * length).astype(jnp.float32)
    weight_fwd = jnp.where(
        (earlier_gap >= 0)[:, None, None], jnp.exp(log_pole[None] * scale_fwd[:, None, None]), 0.0
    )
    weight_bwd = jnp.where(
        (later_gap >= 0)[:, None, None], jnp.exp(log_pole[None] * scale_bwd[:, None, None]), 0.0
    )
    incoming_fwd = jnp.sum(weight_fwd * summaries[0], axis=0)
    incoming_bwd = jnp.sum(weight_bwd * summaries[1], axis=0)
    conv_out = forward_local + carry_term(incoming_fwd, log_pole, residue, length)
    back_conv = (backward_local + carry_term(incoming_bwd, log_pole, residue, length))[::-1]
    filtered = conv_out + skip_gain[None] * product_in
    result = (query_side * filtered).astype(jnp.bfloat16)
    grad_query = upstream * filtered
    grad_product = back_conv + skip_gain[None] * conv_grad
    stream_grads = jnp.concatenate(
        [grad_query, grad_product * value_side, grad_product * key_side], axis=1
    )
    after_rows = from_behind(stream_grads[:tap_reach], "ctx", -1)
    padded = jnp.concatenate([stream_grads, after_rows], axis=0)
    grad_streams = taps_cat[0][None] * padded[:length]
    for offset in range(1, tap_reach + 1):
        grad_streams = grad_streams + taps_cat[offset][None] * padded[offset : offset + length]
    grad_streams = grad_streams.astype(jnp.bfloat16)
    input_grad = lax.psum_scatter(
        jnp.einsum("rk,dk->rd", grad_streams, weight_cat, preferred_element_type=jnp.float32),
        "tp",
        scatter_dimension=0,
        tiled=True,
    )
    return (result, input_grad.astype(jnp.bfloat16))


MESH = pl.DeviceIdType.MESH
SUBLANES = 8
LANES = 128
ROWS = 32
TAIL = 16
VMEM_LIMIT = 60 * 1024 * 1024


def square_partners():
    me = lax.axis_index("tp")
    y, x = me // 2, me % 2
    return me, y * 2 + (1 - x), (1 - y) * 2 + x, (1 - y) * 2 + (1 - x)


def tree_sum(values):
    while len(values) > 1:
        values = [a + b for a, b in zip(values[::2], values[1::2])] + (
            [values[-1]] if len(values) % 2 else []
        )
    return values[0]


def fused_kernel(
    count, tok, w_hbm, taps, rate, res, skip, grad, mixed, out,
    w_buf, held, tails, acc, edge, side, prod, cgrad, conv, back, sgrad, gs, ghead, hrow,
    pole, dsec, dsub_f, dsub_b, gaps, carry_f, carry_b, end_f, end_b, in_f, in_b,
    mine_f, mine_b, all_f, all_b, inc_f, inc_b, out_buf, in_buf, own,
    w_sem, ag_send, ag_recv, nb_send, nb_recv, send_f, recv_f, send_b, recv_b, rs_send, rs_recv,
):
    f32, bf16 = jnp.float32, jnp.bfloat16
    rows, depth = tok.shape
    parts, _, tile = w_buf.shape
    width = grad.shape[1]
    length = grad.shape[0]
    modes = rate.shape[0]
    per_stream = width // tile
    section = rows // SUBLANES
    tiles = width // LANES
    tail, half, quarter, eighth = rows - TAIL, depth // 2, depth // 4, depth // 8
    me, xn, yn, dg = square_partners()
    pos = lax.axis_index("ctx")

    loads = []
    for part in range(parts):
        stream, col = divmod(part, per_stream)
        load = pltpu.make_async_copy(
            w_hbm.at[stream, :, pl.ds(col * tile, tile)], w_buf.at[part], w_sem.at[part]
        )
        load.start()
        loads.append(load)

    barrier = pltpu.get_barrier_semaphore()
    for partner in (xn, yn):
        pl.semaphore_signal(barrier, inc=1, device_id={"tp": partner}, device_id_type=MESH)
    for step in range(1, count):
        pl.semaphore_signal(
            barrier, inc=1, device_id={"ctx": lax.rem(pos + step, count)}, device_id_type=MESH
        )

    def gather(index, source, slot, row, row_count, col, col_count, partner):
        place = (pl.ds(row, row_count), pl.ds(col, col_count))
        return pltpu.make_async_remote_copy(
            src_ref=source.at[place],
            dst_ref=held.at[(slot,) + place],
            send_sem=ag_send.at[index],
            recv_sem=ag_recv.at[index],
            device_id={"tp": partner},
            device_id_type=MESH,
        )

    from_x, from_y = held.at[0], held.at[1]
    copies = [
        gather(0, tok, 0, tail, TAIL, 0, depth, xn),
        gather(1, tok, 1, tail, TAIL, 0, depth, yn),
        gather(2, tok, 0, 0, tail, half, eighth, xn),
        gather(3, tok, 1, 0, tail, 0, eighth, yn),
        gather(4, tok, 0, 0, tail, half + eighth, half - eighth, xn),
        gather(5, tok, 1, 0, tail, eighth, half - eighth, yn),
        gather(6, tok, 0, 0, tail, 0, quarter, xn),
        gather(7, tok, 1, 0, tail, half, quarter, yn),
        gather(8, tok, 0, 0, tail, quarter, quarter, xn),
        gather(9, tok, 1, 0, tail, half + quarter, quarter, yn),
        gather(10, from_y, 2, tail, TAIL, 0, half, xn),
        gather(11, from_x, 2, tail, TAIL, half, half, yn),
    ]
    cuts = [(i * eighth, eighth) for i in range(4)]
    for i, (start, size) in enumerate(cuts):
        copies.append(gather(12 + 2 * i, from_y, 2, 0, tail, start, size, xn))
        copies.append(gather(13 + 2 * i, from_x, 2, 0, tail, half + start, size, yn))

    def to_ctx(index, source, target, partner):
        return pltpu.make_async_remote_copy(
            src_ref=source,
            dst_ref=target,
            send_sem=nb_send.at[index],
            recv_sem=nb_recv.at[index],
            device_id={"ctx": partner},
            device_id_type=MESH,
        )

    after, prior = lax.rem(pos + 1, count), lax.rem(pos + count - 1, count)
    halo = to_ctx(0, edge.at[4], edge.at[0], after)
    side_head = to_ctx(
        1, side.at[:, pl.ds(0, 8), :], side.at[:, pl.ds(length, 8), :], prior
    )
    grad_head = to_ctx(2, grad.at[pl.ds(0, 16), :], ghead, prior)
    has_after, has_prior = pos < count - 1, pos > 0

    pl.semaphore_wait(barrier, 2 + count - 1)
    for index in range(4):
        copies[index].start()

    @pl.when(has_prior)
    def _():
        grad_head.start()

    @pl.when(jnp.logical_not(has_prior))
    def _():
        edge[0] = jnp.zeros((parts, 8, tile), f32)

    @pl.when(jnp.logical_not(has_after))
    def _():
        ghead[...] = jnp.zeros_like(ghead)
        side[:, pl.ds(length, 8), :] = jnp.zeros((3, 8, width), f32)

    pole[...] = jnp.exp(-rate[...])
    for index, steps in enumerate((section, 2 * section, 4 * section, rows)):
        dsec[index] = jnp.exp(rate[...] * (-1.0 * steps))
    sub = lax.broadcasted_iota(jnp.int32, (SUBLANES, LANES), 0)
    subf = lax.broadcasted_iota(jnp.int32, (SUBLANES, width), 0).astype(f32)

    @pl.loop(0, modes)
    def _(n):
        line = rate[pl.ds(n, 1), :]
        dsub_f[n] = jnp.exp(line * (subf * (-1.0 * section)))
        dsub_b[n] = jnp.exp(line * ((SUBLANES - 1.0 - subf) * (-1.0 * section)))

    @pl.loop(0, count)
    def _(g):
        gaps[g] = jnp.exp(rate[...] * (g * (-1 * length)).astype(f32))

    copies[0].wait_recv()
    copies[1].wait_recv()
    copies[10].start()
    copies[11].start()
    for index in range(4, 10):
        copies[index].start()

    def rounded(value):
        return value.astype(bf16).astype(f32)

    def multiply(slot, first, last, *ranges):
        @pl.loop(0, parts)
        def _(part):
            value = None
            for source, start, size in ranges:
                term = jnp.dot(
                    source[:, start : start + size],
                    w_buf[part, start : start + size, :],
                    preferred_element_type=f32,
                )
                value = term if value is None else value + term
            if not first:
                value = acc[slot, part, 8:, :] + value
            acc[slot, part, 8:, :] = rounded(value) if last else value

    for load in loads:
        load.wait()
    multiply(2, True, True, (tok, 0, depth))
    copies[10].wait_recv()
    copies[11].wait_recv()
    tails[0:TAIL] = tok[tail:, :]
    for slot in range(3):
        tails[(slot + 1) * TAIL : (slot + 2) * TAIL] = held[slot, tail:, :]

    @pl.loop(0, parts)
    def _(part):
        value = rounded(jnp.dot(tails[...], w_buf[part], preferred_element_type=f32))
        for slot, owner in enumerate((me, xn, yn, dg)):
            edge[owner + 1, part] = value[(slot + 1) * TAIL - 8 : (slot + 1) * TAIL]

    @pl.when(has_after)
    def _():
        halo.start()

    @pl.when(has_prior)
    def _():
        halo.wait_recv()

    def wide(ref, lanes):
        return [
            jnp.broadcast_to(ref[n : n + 1, lanes], (SUBLANES, LANES)) for n in range(modes)
        ]

    def process(slot, owner):
        base = pl.multiple_of(owner * rows, rows)
        acc[slot, :, 0:8, :] = edge[owner]

        @pl.loop(0, rows // ROWS)
        def _(step):
            start = pl.multiple_of(step * ROWS, ROWS)
            place = pl.ds(pl.multiple_of(base + start, ROWS), ROWS)
            for col in range(0, width, LANES):
                lanes = slice(col, col + LANES)
                mixed_side = []
                for s in range(3):
                    part, inner = s * per_stream + col // tile, col % tile
                    block = acc[slot, part, pl.ds(start, ROWS + 8), inner : inner + LANES]
                    value = taps[s, 0:1, lanes] * block[8:]
                    for j in range(1, 3):
                        value = value + taps[s, j : j + 1, lanes] * block[8 - j : 8 - j + ROWS]
                    side[s, place, lanes] = value
                    mixed_side.append(value)
                prod[col // LANES, place, :] = mixed_side[1] * mixed_side[2]
                cgrad[col // LANES, place, :] = grad[place, lanes].astype(f32) * mixed_side[0]

        @pl.when(jnp.logical_and(owner == 0, has_prior))
        def _():
            side_head.start()

        @pl.loop(0, tiles)
        def _(t):
            lanes = pl.ds(pl.multiple_of(t * LANES, LANES), LANES)
            p = wide(pole, lanes)

            def body(j, state):
                fwd, bwd = state
                x = prod[t, pl.ds(base + j, SUBLANES, stride=section), :]
                y = cgrad[t, pl.ds(base + (section - 1 - j), SUBLANES, stride=section), :]
                return (
                    [a * b + x for a, b in zip(p, fwd)],
                    [a * b + y for a, b in zip(p, bwd)],
                )

            zero = [jnp.zeros((SUBLANES, LANES), f32)] * modes
            fwd, bwd = lax.fori_loop(0, section, body, (zero, zero), unroll=2)
            for n in range(modes):
                residue = res[n : n + 1, lanes]
                ahead, behind = fwd[n] * residue, bwd[n] * residue
                for index, k in enumerate((1, 2, 4)):
                    decay = dsec[index, n : n + 1, lanes]
                    ahead = ahead + jnp.where(sub >= k, decay * pltpu.roll(ahead, k, 0), 0.0)
                    behind = behind + jnp.where(
                        sub < SUBLANES - k, decay * pltpu.roll(behind, SUBLANES - k, 0), 0.0
                    )
                carry_f[owner, n, :, lanes] = jnp.where(sub >= 1, pltpu.roll(ahead, 1, 0), 0.0)
                carry_b[owner, n, :, lanes] = jnp.where(
                    sub < SUBLANES - 1, pltpu.roll(behind, SUBLANES - 1, 0), 0.0
                )
                end_f[owner, n : n + 1, lanes] = ahead[SUBLANES - 1 :]
                end_b[owner, n : n + 1, lanes] = behind[0:1]

    process(2, me)
    copies[2].wait_recv()
    copies[4].wait_recv()
    for i in range(len(cuts)):
        copies[13 + 2 * i].start()
    copies[3].wait_recv()
    copies[5].wait_recv()
    for i in range(len(cuts)):
        copies[12 + 2 * i].start()
    multiply(0, True, False, (from_x, half, half))
    multiply(1, True, False, (from_y, 0, half))
    copies[6].wait_recv()
    multiply(0, False, False, (from_x, 0, quarter))
    copies[7].wait_recv()
    multiply(1, False, False, (from_y, half, quarter))
    copies[8].wait_recv()
    multiply(0, False, True, (from_x, quarter, quarter))
    process(0, xn)
    copies[9].wait_recv()
    multiply(1, False, True, (from_y, half + quarter, quarter))
    process(1, yn)
    opposite = held.at[2]
    for i, (start, size) in enumerate(cuts):
        copies[12 + 2 * i].wait_recv()
        copies[13 + 2 * i].wait_recv()
        multiply(
            2, i == 0, i == len(cuts) - 1, (opposite, start, size), (opposite, half + start, size)
        )
    process(2, dg)

    per_block = dsec[3]
    in_f[0] = jnp.zeros((modes, width), f32)
    in_b[3] = jnp.zeros((modes, width), f32)
    for block in range(4):
        in_f[block + 1] = per_block * in_f[block] + end_f[block]
    for block in (3, 2, 1):
        in_b[block - 1] = per_block * in_b[block] + end_b[block]
    mine_f[...] = in_f[4].astype(bf16)
    mine_b[...] = (per_block * in_b[0] + end_b[0]).astype(bf16)

    def summary(mine, table, send_sem, recv_sem, source, partner):
        return pltpu.make_async_remote_copy(
            src_ref=mine,
            dst_ref=table.at[source],
            send_sem=send_sem.at[partner],
            recv_sem=recv_sem.at[source],
            device_id={"ctx": partner},
            device_id_type=MESH,
        )

    forward = functools.partial(summary, mine_f, all_f, send_f, recv_f)
    backward = functools.partial(summary, mine_b, all_b, send_b, recv_b)
    for step in range(count):
        last = count - 1 - step

        @pl.when(last > pos)
        def _(last=last):
            forward(pos, last).start()

        @pl.when(step < pos)
        def _(step=step):
            backward(pos, step).start()

    @pl.when(has_after)
    def _():
        grad_head.wait_recv()
        side_head.wait_recv()

    inc_f[...] = jnp.zeros_like(inc_f)
    inc_b[...] = jnp.zeros_like(inc_b)
    for other in range(count):

        @pl.when(other < pos)
        def _(other=other):
            forward(other, pos).wait_recv()
            inc_f[...] += gaps[pos - 1 - other] * all_f[other].astype(f32)

        @pl.when(other > pos)
        def _(other=other):
            backward(other, pos).wait_recv()
            inc_b[...] += gaps[other - pos - 1] * all_b[other].astype(f32)

    arrived = inc_f[...]
    for block in range(5):
        in_f[block] = in_f[block] + arrived
        arrived = arrived * per_block
    arrived = inc_b[...]
    for block in (3, 2, 1, 0):
        in_b[block] = in_b[block] + arrived
        arrived = arrived * per_block

    def scan(base, owner, source, target, carry, incoming, shrink, reverse):
        @pl.loop(0, tiles)
        def _(t):
            lanes = pl.ds(pl.multiple_of(t * LANES, LANES), LANES)
            p, r = wide(pole, lanes), wide(res, lanes)

            def body(i, state):
                j = section - 1 - i if reverse else i
                place = pl.ds(base + j, SUBLANES, stride=section)
                x = source[t, place, :]
                state = [a * b + c * x for a, b, c in zip(p, state, r)]
                target[t, place, :] = tree_sum(state)
                return state

            start = [
                carry[owner, n, :, lanes]
                + shrink[n, :, lanes] * incoming[owner, n : n + 1, lanes]
                for n in range(modes)
            ]
            lax.fori_loop(0, section, body, start, unroll=2)

    def heads(owner):
        @pl.when(owner == 3)
        def _():
            hrow[...] = ghead[...].astype(f32)[0:8]

        @pl.when(owner < 3)
        def _():
            hrow[...] = grad[pl.ds(pl.multiple_of((owner + 1) * rows, rows), 16), :].astype(f32)[0:8]

        place = pl.ds(pl.multiple_of((owner + 1) * rows, rows), 8)
        for col in range(0, width, LANES):
            lanes = slice(col, col + LANES)
            q, k, v = (side[s, place, lanes] for s in range(3))
            g = hrow[:, lanes]
            x, cg = k * v, g * q
            p, r = pole[:, lanes], res[:, lanes]
            ahead, behind = p * in_f[owner + 1, :, lanes], in_b[owner, :, lanes]

            def total(value):
                return jnp.sum(value, axis=0, keepdims=True)

            first = sub == 0
            conv_head = jnp.where(first, total(ahead), total(p * ahead) + total(r * p) * x[0:1])
            conv_head = conv_head + total(r) * x
            back_head = jnp.where(
                first, total(behind), total(behind / p) - total(r / p) * cg[0:1]
            )
            gain = skip[0:1, lanes]
            filtered = conv_head + gain * x
            product = back_head + gain * cg
            for s, value in enumerate((g * filtered, product * v, product * k)):
                sgrad[rows:, s * width + col : s * width + col + LANES] = value

    def finish_block(owner):
        base = pl.multiple_of(owner * rows, rows)
        scan(base, owner, prod, conv, carry_f, in_f, dsub_f, False)
        scan(base, owner, cgrad, back, carry_b, in_b, dsub_b, True)
        heads(owner)

        @pl.loop(0, rows // ROWS)
        def _(step):
            start = pl.multiple_of(step * ROWS, ROWS)
            here = pl.ds(start, ROWS)
            place = pl.ds(pl.multiple_of(base + start, ROWS), ROWS)
            for col in range(0, width, LANES):
                lanes = slice(col, col + LANES)
                gain = skip[0:1, lanes]
                filtered = conv[col // LANES, place, :] + gain * prod[col // LANES, place, :]
                mixed[place, lanes] = (side[0, place, lanes] * filtered).astype(bf16)
                product = back[col // LANES, place, :] + gain * cgrad[col // LANES, place, :]
                upstream = grad[place, lanes].astype(f32)
                sgrad[here, lanes] = upstream * filtered
                sgrad[here, width + col : width + col + LANES] = product * side[2, place, lanes]
                sgrad[here, 2 * width + col : 2 * width + col + LANES] = (
                    product * side[1, place, lanes]
                )

        @pl.loop(0, rows // ROWS)
        def _(step):
            start = pl.multiple_of(step * ROWS, ROWS)
            place = pl.ds(pl.multiple_of(base + start, ROWS), ROWS)
            for s in range(3):
                for col in range(0, width, LANES):
                    lanes = slice(s * width + col, s * width + col + LANES)
                    block = sgrad[pl.ds(start, ROWS + 8), lanes]
                    value = taps[s, 0:1, col : col + LANES] * block[:ROWS]
                    for j in range(1, 3):
                        value = value + taps[s, j : j + 1, col : col + LANES] * block[j : j + ROWS]
                    gs[place, lanes] = value.astype(bf16)

    _, pieces, _, cols = out_buf.shape
    split = pieces // 2

    def send(kind, piece, partner):
        return pltpu.make_async_remote_copy(
            src_ref=out_buf.at[kind, piece],
            dst_ref=in_buf.at[kind, piece],
            send_sem=rs_send.at[kind, piece],
            recv_sem=rs_recv.at[kind, piece],
            device_id={"tp": partner},
            device_id_type=MESH,
        )

    def partial(owner, piece):
        block = pl.ds(pl.multiple_of(owner * rows, rows), rows)
        here = pl.ds(pl.multiple_of(piece * cols, cols), cols)
        total = None
        for part in range(parts):
            term = lax.dot_general(
                gs[block, part * tile : (part + 1) * tile],
                w_buf[part, here, :],
                (((1,), (1,)), ((), ())),
                preferred_element_type=f32,
            )
            total = term if total is None else total + term
        return total

    def emit(kind, piece, value, partner):
        out_buf[kind, piece] = value.astype(bf16)
        send(kind, piece, partner).start()

    finish_block(dg)

    @pl.loop(0, split)
    def _(k):
        emit(0, k, partial(dg, k), xn)
        emit(0, split + k, partial(dg, split + k), yn)

    finish_block(xn)
    finish_block(yn)

    @pl.loop(0, split)
    def _(k):
        emit(1, k, partial(xn, k), xn)
        emit(2, split + k, partial(yn, split + k), yn)

    @pl.loop(0, split)
    def _(k):
        own_x, own_y = partial(xn, split + k), partial(yn, k)
        send(0, split + k, yn).wait_recv()
        emit(1, split + k, own_x + in_buf[0, split + k].astype(f32), xn)
        send(0, k, xn).wait_recv()
        emit(2, k, own_y + in_buf[0, k].astype(f32), yn)

    finish_block(me)

    @pl.loop(0, pieces)
    def _(k):
        own[k] = partial(me, k)

    for k in [k + offset for k in range(split) for offset in (0, split)]:
        send(1, k, xn).wait_recv()
        send(2, k, yn).wait_recv()
        out[:, k * cols : (k + 1) * cols] = (
            own[k] + in_buf[1, k].astype(f32) + in_buf[2, k].astype(f32)
        ).astype(bf16)

    for copy in copies:
        copy.wait_send()
    for k in range(pieces):
        send(0, k, xn if k < split else yn).wait_send()
        send(1, k, xn).wait_send()
        send(2, k, yn).wait_send()

    @pl.when(has_after)
    def _():
        halo.wait_send()

    @pl.when(has_prior)
    def _():
        side_head.wait_send()
        grad_head.wait_send()

    for other in range(count):

        @pl.when(other > pos)
        def _(other=other):
            forward(pos, other).wait_send()

        @pl.when(other < pos)
        def _(other=other):
            backward(pos, other).wait_send()


def square_shards(tokens, in_weight, short_taps, decay_rate, residue, skip_gain, grad_out):
    count = lax.axis_size("ctx")
    rows, depth = tokens.shape
    streams, _, width = in_weight.shape
    length = 4 * rows
    modes = decay_rate.shape[0]
    tile = min(256, width)
    parts = streams * (width // tile)
    pieces = 8
    f32, bf16 = jnp.float32, jnp.bfloat16
    vmem, dma = pltpu.VMEM, pltpu.SemaphoreType.DMA
    table = vmem((modes, width), f32)
    plane = vmem((width // LANES, length, LANES), f32)
    fan = vmem((modes, SUBLANES, width), f32)
    carry = vmem((4, modes, SUBLANES, width), f32)
    ends = vmem((4, modes, width), f32)
    travelling = vmem((3, pieces, rows, depth // pieces), bf16)
    inner = pl.BlockSpec(memory_space=pltpu.VMEM)
    return pl.pallas_call(
        functools.partial(fused_kernel, count),
        out_shape=(
            jax.ShapeDtypeStruct((length, width), bf16),
            jax.ShapeDtypeStruct((rows, depth), bf16),
        ),
        in_specs=[inner, pl.BlockSpec(memory_space=pl.ANY)] + [inner] * 5,
        out_specs=(inner, inner),
        scratch_shapes=[
            vmem((parts, depth, tile), bf16),
            vmem((3, rows, depth), bf16),
            vmem((4 * TAIL, depth), bf16),
            vmem((3, parts, rows + 8, tile), f32),
            vmem((5, parts, 8, tile), f32),
            vmem((3, length + 8, width), f32),
            plane, plane, plane, plane,
            vmem((rows + 8, streams * width), f32),
            vmem((length, streams * width), bf16),
            vmem((16, width), bf16),
            vmem((8, width), f32),
            table,
            ends, fan, fan,
            vmem((count, modes, width), f32),
            carry, carry, ends, ends,
            vmem((5, modes, width), f32),
            ends,
            vmem((modes, width), bf16),
            vmem((modes, width), bf16),
            vmem((count, modes, width), bf16),
            vmem((count, modes, width), bf16),
            table, table,
            travelling, travelling,
            vmem((pieces, rows, depth // pieces), f32),
            dma((parts,)), dma((20,)), dma((20,)), dma((3,)), dma((3,)),
            dma((count,)), dma((count,)), dma((count,)), dma((count,)),
            dma((3, pieces)), dma((3, pieces)),
        ],
        compiler_params=pltpu.CompilerParams(
            collective_id=0, has_side_effects=True, vmem_limit_bytes=VMEM_LIMIT
        ),
    )(tokens, in_weight, short_taps, decay_rate, residue, skip_gain[None], grad_out)


def solution(mesh):
    in_specs = (
        P(("ctx", "tp"), None),
        P(None, None, "tp"),
        P(None, None, "tp"),
        P(None, "tp"),
        P(None, "tp"),
        P("tp"),
        P("ctx", "tp"),
    )
    out_specs = (P("ctx", "tp"), P(("ctx", "tp"), None))
    body = square_shards if mesh.shape["tp"] == 4 else shards
    return jax.shard_map(body, mesh=mesh, in_specs=in_specs, out_specs=out_specs, check_vma=False)
```

time: 114 us -> 97.3 us (0.85)
  Pallas kernels: 110 us -> 92.3 us
  local copies, waits for them, and re-layouts: 2.38 us -> 4.16 us
    pallas_call x3 -> x1, Pallas kernels: 110 us -> 92.3 us  [square_shards(): pl.pallas_call(functools.partial(fused_kernel, count), out_shape=(jax.Sha...]
    unnamed x6 -> x2, local copies, waits for them, and re-layouts: 2.38 us -> 4.16 us
where the time goes in v1:
time: 97.3 us; the launch traced here: 97.1 us
  Pallas kernels  92.3 us (95%)
  local copies, waits for them, and re-layouts  4.16 us (4%)
    pallas_call x1, Pallas kernels, square_shards(): pl.pallas_call(functools.partial(fused_kernel, count), out_shape=(jax.Sha...  92.3 us
    unnamed x2, local copies, waits for them, and re-layouts  4.16 us

profile of v1, /device:TPU:0, one launch (start us, length us, event | category | flops | bytes accessed | tf_op | source)
XLA Modules:
  0.0 97.1 jit_solution(8257081478787093016)
XLA Ops:
  0.6 92.3 %shard_map.86 = (bf16[512,512]{1,0:T(8,128)(2,1)}, bf16[128,4096]{1,0:T(8,128)(2,1)}) custom-call(bf16[128,4096]{1,0:T(8,128)(2,1)} %tok.1, bf16[3,4096,512]{2,1,0:T(8,128)(2,1)} %w_hbm.1, f32[3,3,512]{2,1,0:T(4,128)} %taps.1, f32[16,512]{1,0:T(8,128)} %rate.1, f32[16,512]{1,0:T(8,128)} %res.1, f32[1,512]{1,0:T(1,128)} %bitcast.1, bf16[512,512]{1,0:T(8,128)(2,1)} %grad.1), custom_call_target="tpu_custom_call" | custom-call | tf_op jit(solution)/shard_map/pallas_call | solution.py:675
  92.9 1.9 %copy.11 = bf16[512,512]{1,0:T(8,128)(2,1)} copy(bf16[512,512]{1,0:T(8,128)(2,1)} %get-tuple-element.4) | data formatting | bytes 1048576
  94.8 2.3 %copy.12 = bf16[128,4096]{1,0:T(8,128)(2,1)} copy(bf16[128,4096]{1,0:T(8,128)(2,1)} %get-tuple-element.5) | data formatting | bytes 2097152

commit v2 on v1

--- a/solution.py
+++ b/solution.py
@@ -149,11 +149,11 @@
 
 
 def fused_kernel(
-    count, tok, w_hbm, taps, rate, res, skip, grad, mixed, out,
-    w_buf, held, tails, acc, edge, side, prod, cgrad, conv, back, sgrad, gs, ghead, hrow,
-    pole, dsec, dsub_f, dsub_b, gaps, carry_f, carry_b, end_f, end_b, in_f, in_b,
+    count, tok_hbm, w_hbm, taps_hbm, rate_hbm, res_hbm, skip_hbm, grad_hbm, mixed, out,
+    tok, taps, rate, res, skip, grad, w_buf, held, tails, acc, edge, side, prod, cgrad, conv, back, sgrad, gs, ghead, hrow,
+    pole, dsec, dsub_f, dsub_b, gaps, carry_f, carry_b, end_f, end_b, in_f, in_b, new_f, new_b,
     mine_f, mine_b, all_f, all_b, inc_f, inc_b, out_buf, in_buf, own,
-    w_sem, ag_send, ag_recv, nb_send, nb_recv, send_f, recv_f, send_b, recv_b, rs_send, rs_recv,
+    in_sem, w_sem, ag_send, ag_recv, nb_send, nb_recv, send_f, recv_f, send_b, recv_b, rs_send, rs_recv,
 ):
     f32, bf16 = jnp.float32, jnp.bfloat16
     rows, depth = tok.shape
@@ -168,6 +168,24 @@
     me, xn, yn, dg = square_partners()
     pos = lax.axis_index("ctx")
 
+    barrier = pltpu.get_barrier_semaphore()
+    for partner in (xn, yn):
+        pl.semaphore_signal(barrier, inc=1, device_id={"tp": partner}, device_id_type=MESH)
+    for step in range(1, count):
+        pl.semaphore_signal(
+            barrier, inc=1, device_id={"ctx": lax.rem(pos + step, count)}, device_id_type=MESH
+        )
+
+    pairs = (
+        (rate_hbm, rate), (res_hbm, res), (taps_hbm, taps), (skip_hbm, skip),
+        (tok_hbm, tok), (grad_hbm, grad),
+    )
+    inputs = [
+        pltpu.make_async_copy(source, target, in_sem.at[index])
+        for index, (source, target) in enumerate(pairs)
+    ]
+    for load in inputs:
+        load.start()
     loads = []
     for part in range(parts):
         stream, col = divmod(part, per_stream)
@@ -176,14 +194,6 @@
         )
         load.start()
         loads.append(load)
-
-    barrier = pltpu.get_barrier_semaphore()
-    for partner in (xn, yn):
-        pl.semaphore_signal(barrier, inc=1, device_id={"tp": partner}, device_id_type=MESH)
-    for step in range(1, count):
-        pl.semaphore_signal(
-            barrier, inc=1, device_id={"ctx": lax.rem(pos + step, count)}, device_id_type=MESH
-        )
 
     def gather(index, source, slot, row, row_count, col, col_count, partner):
         place = (pl.ds(row, row_count), pl.ds(col, col_count))
@@ -198,20 +208,21 @@
 
     from_x, from_y = held.at[0], held.at[1]
     copies = [
-        gather(0, tok, 0, tail, TAIL, 0, depth, xn),
-        gather(1, tok, 1, tail, TAIL, 0, depth, yn),
-        gather(2, tok, 0, 0, tail, half, eighth, xn),
-        gather(3, tok, 1, 0, tail, 0, eighth, yn),
-        gather(4, tok, 0, 0, tail, half + eighth, half - eighth, xn),
-        gather(5, tok, 1, 0, tail, eighth, half - eighth, yn),
-        gather(6, tok, 0, 0, tail, 0, quarter, xn),
-        gather(7, tok, 1, 0, tail, half, quarter, yn),
-        gather(8, tok, 0, 0, tail, quarter, quarter, xn),
-        gather(9, tok, 1, 0, tail, half + quarter, quarter, yn),
+        gather(0, tok_hbm, 0, tail, TAIL, 0, depth, xn),
+        gather(1, tok_hbm, 1, tail, TAIL, 0, depth, yn),
+        gather(2, tok_hbm, 0, 0, tail, half, eighth, xn),
+        gather(3, tok_hbm, 1, 0, tail, 0, eighth, yn),
+        gather(4, tok_hbm, 0, 0, tail, half + eighth, half - eighth, xn),
+        gather(5, tok_hbm, 1, 0, tail, eighth, half - eighth, yn),
+        gather(6, tok_hbm, 0, 0, tail, 0, quarter, xn),
+        gather(7, tok_hbm, 1, 0, tail, half, quarter, yn),
+        gather(8, tok_hbm, 0, 0, tail, quarter, quarter, xn),
+        gather(9, tok_hbm, 1, 0, tail, half + quarter, quarter, yn),
         gather(10, from_y, 2, tail, TAIL, 0, half, xn),
         gather(11, from_x, 2, tail, TAIL, half, half, yn),
     ]
-    cuts = [(i * eighth, eighth) for i in range(4)]
+    sixteenth = eighth // 2
+    cuts = [(0, 3 * sixteenth), (3 * sixteenth, eighth), (5 * sixteenth, eighth), (7 * sixteenth, sixteenth)]
     for i, (start, size) in enumerate(cuts):
         copies.append(gather(12 + 2 * i, from_y, 2, 0, tail, start, size, xn))
         copies.append(gather(13 + 2 * i, from_x, 2, 0, tail, half + start, size, yn))
@@ -231,7 +242,7 @@
     side_head = to_ctx(
         1, side.at[:, pl.ds(0, 8), :], side.at[:, pl.ds(length, 8), :], prior
     )
-    grad_head = to_ctx(2, grad.at[pl.ds(0, 16), :], ghead, prior)
+    grad_head = to_ctx(2, grad_hbm.at[pl.ds(0, 16), :], ghead, prior)
     has_after, has_prior = pos < count - 1, pos > 0
 
     pl.semaphore_wait(barrier, 2 + count - 1)
@@ -251,6 +262,8 @@
         ghead[...] = jnp.zeros_like(ghead)
         side[:, pl.ds(length, 8), :] = jnp.zeros((3, 8, width), f32)
 
+    for load in inputs:
+        load.wait()
     pole[...] = jnp.exp(-rate[...])
     for index, steps in enumerate((section, 2 * section, 4 * section, rows)):
         dsec[index] = jnp.exp(rate[...] * (-1.0 * steps))
@@ -377,6 +390,52 @@
                 )
                 end_f[owner, n : n + 1, lanes] = ahead[SUBLANES - 1 :]
                 end_b[owner, n : n + 1, lanes] = behind[0:1]
+
+    def scan(base, owner, source, target, carry, incoming, shrink, reverse):
+        @pl.loop(0, tiles)
+        def _(t):
+            lanes = pl.ds(pl.multiple_of(t * LANES, LANES), LANES)
+            p, r = wide(pole, lanes), wide(res, lanes)
+
+            def body(i, state):
+                j = section - 1 - i if reverse else i
+                place = pl.ds(base + j, SUBLANES, stride=section)
+                x = source[t, place, :]
+                state = [a * b + c * x for a, b, c in zip(p, state, r)]
+                target[t, place, :] = tree_sum(state)
+                return state
+
+            start = [
+                carry[owner, n, :, lanes]
+                + shrink[n, :, lanes] * incoming[owner, n : n + 1, lanes]
+                for n in range(modes)
+            ]
+            lax.fori_loop(0, section, body, start, unroll=2)
+
+    def finish_scan(owner):
+        base = pl.multiple_of(owner * rows, rows)
+        scan(base, owner, prod, conv, carry_f, in_f, dsub_f, False)
+        scan(base, owner, cgrad, back, carry_b, in_b, dsub_b, True)
+
+    def add_arrived(owner, target, incoming, shrink, reverse):
+        base = pl.multiple_of(owner * rows, rows)
+
+        @pl.loop(0, tiles)
+        def _(t):
+            lanes = pl.ds(pl.multiple_of(t * LANES, LANES), LANES)
+            p = wide(pole, lanes)
+
+            def body(i, state):
+                j = section - 1 - i if reverse else i
+                place = pl.ds(base + j, SUBLANES, stride=section)
+                state = [a * b for a, b in zip(p, state)]
+                target[t, place, :] = target[t, place, :] + tree_sum(state)
+                return state
+
+            start = [
+                shrink[n, :, lanes] * incoming[owner, n : n + 1, lanes] for n in range(modes)
+            ]
+            lax.fori_loop(0, section, body, start, unroll=2)
 
     process(2, me)
     copies[2].wait_recv()
@@ -441,6 +500,8 @@
         def _(step=step):
             backward(pos, step).start()
 
+    finish_scan(dg)
+
     @pl.when(has_after)
     def _():
         grad_head.wait_recv()
@@ -463,32 +524,15 @@
     arrived = inc_f[...]
     for block in range(5):
         in_f[block] = in_f[block] + arrived
+        new_f[block] = arrived
         arrived = arrived * per_block
     arrived = inc_b[...]
     for block in (3, 2, 1, 0):
         in_b[block] = in_b[block] + arrived
+        new_b[block] = arrived
         arrived = arrived * per_block
-
-    def scan(base, owner, source, target, carry, incoming, shrink, reverse):
-        @pl.loop(0, tiles)
-        def _(t):
-            lanes = pl.ds(pl.multiple_of(t * LANES, LANES), LANES)
-            p, r = wide(pole, lanes), wide(res, lanes)
-
-            def body(i, state):
-                j = section - 1 - i if reverse else i
-                place = pl.ds(base + j, SUBLANES, stride=section)
-                x = source[t, place, :]
-                state = [a * b + c * x for a, b, c in zip(p, state, r)]
-                target[t, place, :] = tree_sum(state)
-                return state
-
-            start = [
-                carry[owner, n, :, lanes]
-                + shrink[n, :, lanes] * incoming[owner, n : n + 1, lanes]
-                for n in range(modes)
-            ]
-            lax.fori_loop(0, section, body, start, unroll=2)
+    add_arrived(dg, conv, new_f, dsub_f, False)
+    add_arrived(dg, back, new_b, dsub_b, True)
 
     def heads(owner):
         @pl.when(owner == 3)
@@ -525,8 +569,6 @@
 
     def finish_block(owner):
         base = pl.multiple_of(owner * rows, rows)
-        scan(base, owner, prod, conv, carry_f, in_f, dsub_f, False)
-        scan(base, owner, cgrad, back, carry_b, in_b, dsub_b, True)
         heads(owner)
 
         @pl.loop(0, rows // ROWS)
@@ -598,7 +640,9 @@
         emit(0, k, partial(dg, k), xn)
         emit(0, split + k, partial(dg, split + k), yn)
 
+    finish_scan(xn)
     finish_block(xn)
+    finish_scan(yn)
     finish_block(yn)
 
     @pl.loop(0, split)
@@ -614,6 +658,7 @@
         send(0, k, xn).wait_recv()
         emit(2, k, own_y + in_buf[0, k].astype(f32), yn)
 
+    finish_scan(me)
     finish_block(me)
 
     @pl.loop(0, pieces)
@@ -652,6 +697,28 @@
         @pl.when(other < pos)
         def _(other=other):
             backward(pos, other).wait_send()
+
+
+def hand_over_kernel(mixed, grads, mixed_out, grads_out, sem):
+    copies = [
+        pltpu.make_async_copy(mixed, mixed_out, sem.at[0]),
+        pltpu.make_async_copy(grads, grads_out, sem.at[1]),
+    ]
+    for copy in copies:
+        copy.start()
+    for copy in copies:
+        copy.wait()
+
+
+def hand_over(results):
+    return pl.pallas_call(
+        hand_over_kernel,
+        out_shape=tuple(jax.ShapeDtypeStruct(a.shape, a.dtype) for a in results),
+        in_specs=[pl.BlockSpec(memory_space=pltpu.VMEM)] * 2,
+        out_specs=(pl.BlockSpec(memory_space=pl.ANY),) * 2,
+        scratch_shapes=[pltpu.SemaphoreType.DMA((2,))],
+        compiler_params=pltpu.CompilerParams(vmem_limit_bytes=4 * 1024 * 1024),
+    )(*results)
 
 
 def square_shards(tokens, in_weight, short_taps, decay_rate, residue, skip_gain, grad_out):
@@ -672,15 +739,20 @@
     ends = vmem((4, modes, width), f32)
     travelling = vmem((3, pieces, rows, depth // pieces), bf16)
     inner = pl.BlockSpec(memory_space=pltpu.VMEM)
-    return pl.pallas_call(
+    results = pl.pallas_call(
         functools.partial(fused_kernel, count),
         out_shape=(
-            jax.ShapeDtypeStruct((length, width), bf16),
-            jax.ShapeDtypeStruct((rows, depth), bf16),
+            pltpu.VMEM((length, width), bf16),
+            pltpu.VMEM((rows, depth), bf16),
         ),
-        in_specs=[inner, pl.BlockSpec(memory_space=pl.ANY)] + [inner] * 5,
+        in_specs=[pl.BlockSpec(memory_space=pl.ANY)] * 7,
         out_specs=(inner, inner),
         scratch_shapes=[
+            vmem((rows, depth), bf16),
+            vmem(short_taps.shape, f32),
+            table, table,
+            vmem((1, width), f32),
+            vmem((length, width), bf16),
             vmem((parts, depth, tile), bf16),
             vmem((3, rows, depth), bf16),
             vmem((4 * TAIL, depth), bf16),
@@ -698,6 +770,8 @@
             carry, carry, ends, ends,
             vmem((5, modes, width), f32),
             ends,
+            vmem((5, modes, width), f32),
+            ends,
             vmem((modes, width), bf16),
             vmem((modes, width), bf16),
             vmem((count, modes, width), bf16),
@@ -705,7 +779,7 @@
             table, table,
             travelling, travelling,
             vmem((pieces, rows, depth // pieces), f32),
-            dma((parts,)), dma((20,)), dma((20,)), dma((3,)), dma((3,)),
+            dma((6,)), dma((parts,)), dma((20,)), dma((20,)), dma((3,)), dma((3,)),
             dma((count,)), dma((count,)), dma((count,)), dma((count,)),
             dma((3, pieces)), dma((3, pieces)),
         ],
@@ -713,6 +787,7 @@
             collective_id=0, has_side_effects=True, vmem_limit_bytes=VMEM_LIMIT
         ),
     )(tokens, in_weight, short_taps, decay_rate, residue, skip_gain[None], grad_out)
+    return hand_over(results)
 
 
 def solution(mesh):

time: 97.3 us -> 91.4 us (0.939)
  local copies, waits for them, and re-layouts: 4.16 us -> 0 us
  Pallas kernels: 92.3 us -> 90.6 us
    unnamed x2 -> x0, local copies, waits for them, and re-layouts: 4.16 us -> none
    pallas_call x1 -> x2, Pallas kernels: 92.3 us -> 90.6 us  [the longest x1 89.5 us: square_shards(): pl.pallas_call(functools.partial(fused_kernel, count), out_shape=(pltpu.V...]
where the time goes in v2:
time: 91.4 us; the launch traced here: 91.3 us
  Pallas kernels  90.6 us (99%)
    pallas_call x1, Pallas kernels, square_shards(): pl.pallas_call(functools.partial(fused_kernel, count), out_shape=(pltpu.V...  89.5 us

profile of v2, /device:TPU:0, one launch (start us, length us, event | category | flops | bytes accessed | tf_op | source)
XLA Modules:
  0.0 91.3 jit_solution(534972006927653164)
XLA Ops:
  0.6 89.5 %shard_map.86 = (bf16[512,512]{1,0:T(8,128)(2,1)S(1)}, bf16[128,4096]{1,0:T(8,128)(2,1)S(1)}) custom-call(bf16[128,4096]{1,0:T(8,128)(2,1)} %tok_hbm.1, bf16[3,4096,512]{2,1,0:T(8,128)(2,1)} %w_hbm.1, f32[3,3,512]{2,1,0:T(4,128)} %taps_hbm.1, f32[16,512]{1,0:T(8,128)} %rate_hbm.1, f32[16,512]{1,0:T(8,128)} %res_hbm.1, f32[1,512]{1,0:T(1,128)} %bitcast.1, ...), custom_call_target="tpu_custom_call" | custom-call | tf_op jit(solution)/shard_map/pallas_call | solution.py:742
  90.1 1.2 %shard_map.87 = (bf16[512,512]{1,0:T(8,128)(2,1)}, bf16[128,4096]{1,0:T(8,128)(2,1)}) custom-call(bf16[512,512]{1,0:T(8,128)(2,1)S(1)} %get-tuple-element.4.mixed, bf16[128,4096]{1,0:T(8,128)(2,1)S(1)} %get-tuple-element.5.grads), custom_call_target="tpu_custom_call" | custom-call | tf_op jit(solution)/shard_map/pallas_call | solution.py:714

commit v3 on v2

--- a/solution.py
+++ b/solution.py
@@ -150,13 +150,13 @@
 
 def fused_kernel(
     count, tok_hbm, w_hbm, taps_hbm, rate_hbm, res_hbm, skip_hbm, grad_hbm, mixed, out,
-    tok, taps, rate, res, skip, grad, w_buf, held, tails, acc, edge, side, prod, cgrad, conv, back, sgrad, gs, ghead, hrow,
+    tok, taps, rate, res, skip, grad, w_buf, held, acc, edge, side, prod, cgrad, conv, back, sgrad, gs, ghead, hrow,
     pole, dsec, dsub_f, dsub_b, gaps, carry_f, carry_b, end_f, end_b, in_f, in_b, new_f, new_b,
     mine_f, mine_b, all_f, all_b, inc_f, inc_b, out_buf, in_buf, own,
     in_sem, w_sem, ag_send, ag_recv, nb_send, nb_recv, send_f, recv_f, send_b, recv_b, rs_send, rs_recv,
 ):
     f32, bf16 = jnp.float32, jnp.bfloat16
-    rows, depth = tok.shape
+    rows, depth = tok_hbm.shape
     parts, _, tile = w_buf.shape
     width = grad.shape[1]
     length = grad.shape[0]
@@ -178,7 +178,7 @@
 
     pairs = (
         (rate_hbm, rate), (res_hbm, res), (taps_hbm, taps), (skip_hbm, skip),
-        (tok_hbm, tok), (grad_hbm, grad),
+        (tok_hbm, tok.at[pl.ds(0, rows)]), (grad_hbm, grad),
     )
     inputs = [
         pltpu.make_async_copy(source, target, in_sem.at[index])
@@ -212,20 +212,25 @@
         gather(1, tok_hbm, 1, tail, TAIL, 0, depth, yn),
         gather(2, tok_hbm, 0, 0, tail, half, eighth, xn),
         gather(3, tok_hbm, 1, 0, tail, 0, eighth, yn),
-        gather(4, tok_hbm, 0, 0, tail, half + eighth, half - eighth, xn),
-        gather(5, tok_hbm, 1, 0, tail, eighth, half - eighth, yn),
+        gather(4, tok_hbm, 0, 0, tail, half + eighth, eighth, xn),
+        gather(5, tok_hbm, 1, 0, tail, eighth, eighth, yn),
         gather(6, tok_hbm, 0, 0, tail, 0, quarter, xn),
         gather(7, tok_hbm, 1, 0, tail, half, quarter, yn),
-        gather(8, tok_hbm, 0, 0, tail, quarter, quarter, xn),
-        gather(9, tok_hbm, 1, 0, tail, half + quarter, quarter, yn),
-        gather(10, from_y, 2, tail, TAIL, 0, half, xn),
-        gather(11, from_x, 2, tail, TAIL, half, half, yn),
+        gather(8, tok_hbm, 0, 0, tail, half + quarter, quarter, xn),
+        gather(9, tok_hbm, 1, 0, tail, quarter, quarter, yn),
+        gather(10, tok_hbm, 0, 0, tail, quarter, quarter, xn),
+        gather(11, tok_hbm, 1, 0, tail, half + quarter, quarter, yn),
+        gather(12, from_y, 2, tail, TAIL, 0, half, xn),
+        gather(13, from_x, 2, tail, TAIL, half, half, yn),
     ]
     sixteenth = eighth // 2
-    cuts = [(0, 3 * sixteenth), (3 * sixteenth, eighth), (5 * sixteenth, eighth), (7 * sixteenth, sixteenth)]
+    cuts = [
+        (0, quarter), (quarter, eighth),
+        (quarter + eighth, sixteenth), (half - sixteenth, sixteenth),
+    ]
     for i, (start, size) in enumerate(cuts):
-        copies.append(gather(12 + 2 * i, from_y, 2, 0, tail, start, size, xn))
-        copies.append(gather(13 + 2 * i, from_x, 2, 0, tail, half + start, size, yn))
+        copies.append(gather(14 + 2 * i, from_y, 2, 0, tail, start, size, xn))
+        copies.append(gather(15 + 2 * i, from_x, 2, 0, tail, half + start, size, yn))
 
     def to_ctx(index, source, target, partner):
         return pltpu.make_async_remote_copy(
@@ -282,9 +287,9 @@
 
     copies[0].wait_recv()
     copies[1].wait_recv()
-    copies[10].start()
-    copies[11].start()
-    for index in range(4, 10):
+    copies[12].start()
+    copies[13].start()
+    for index in range(4, 8):
         copies[index].start()
 
     def rounded(value):
@@ -305,20 +310,22 @@
                 value = acc[slot, part, 8:, :] + value
             acc[slot, part, 8:, :] = rounded(value) if last else value
 
+    copies[12].wait_recv()
+    copies[13].wait_recv()
+    for slot in range(3):
+        tok[rows + slot * TAIL : rows + (slot + 1) * TAIL] = held[slot, tail:, :]
     for load in loads:
         load.wait()
-    multiply(2, True, True, (tok, 0, depth))
-    copies[10].wait_recv()
-    copies[11].wait_recv()
-    tails[0:TAIL] = tok[tail:, :]
-    for slot in range(3):
-        tails[(slot + 1) * TAIL : (slot + 2) * TAIL] = held[slot, tail:, :]
+    copies[8].start()
+    copies[9].start()
 
     @pl.loop(0, parts)
     def _(part):
-        value = rounded(jnp.dot(tails[...], w_buf[part], preferred_element_type=f32))
+        value = rounded(jnp.dot(tok[...], w_buf[part], preferred_element_type=f32))
+        acc[2, part, 8:, :] = value[:rows]
         for slot, owner in enumerate((me, xn, yn, dg)):
-            edge[owner + 1, part] = value[(slot + 1) * TAIL - 8 : (slot + 1) * TAIL]
+            end = rows + slot * TAIL
+            edge[owner + 1, part] = value[end - 8 : end]
 
     @pl.when(has_after)
     def _():
@@ -437,31 +444,51 @@
             ]
             lax.fori_loop(0, section, body, start, unroll=2)
 
+    def multiply_pair(first, *ranges):
+        @pl.loop(0, parts)
+        def _(part):
+            value = None
+            for start, size in ranges:
+                both = held[0:2, :, start : start + size].reshape(2 * rows, size)
+                term = jnp.dot(
+                    both, w_buf[part, start : start + size, :], preferred_element_type=f32
+                )
+                value = term if value is None else value + term
+            for slot in range(2):
+                here = value[slot * rows : (slot + 1) * rows]
+                acc[slot, part, 8:, :] = (
+                    here if first else rounded(acc[slot, part, 8:, :] + here)
+                )
+
+    copies[10].start()
+    copies[11].start()
     process(2, me)
-    copies[2].wait_recv()
-    copies[4].wait_recv()
-    for i in range(len(cuts)):
-        copies[13 + 2 * i].start()
-    copies[3].wait_recv()
-    copies[5].wait_recv()
-    for i in range(len(cuts)):
-        copies[12 + 2 * i].start()
-    multiply(0, True, False, (from_x, half, half))
-    multiply(1, True, False, (from_y, 0, half))
-    copies[6].wait_recv()
-    multiply(0, False, False, (from_x, 0, quarter))
-    copies[7].wait_recv()
-    multiply(1, False, False, (from_y, half, quarter))
+    for index in (2, 4):
+        copies[index].wait_recv()
+    copies[15].start()
+    for index in (3, 5):
+        copies[index].wait_recv()
+    copies[14].start()
+    for index in (6, 7):
+        copies[index].wait_recv()
+    multiply_pair(True, (0, quarter), (half, quarter))
     copies[8].wait_recv()
-    multiply(0, False, True, (from_x, quarter, quarter))
+    copies[17].start()
+    copies[9].wait_recv()
+    copies[16].start()
+    for index in (10, 11):
+        copies[index].wait_recv()
+    multiply_pair(False, (quarter, quarter), (half + quarter, quarter))
+    copies[18].start()
+    copies[19].start()
     process(0, xn)
-    copies[9].wait_recv()
-    multiply(1, False, True, (from_y, half + quarter, quarter))
     process(1, yn)
+    copies[20].start()
+    copies[21].start()
     opposite = held.at[2]
     for i, (start, size) in enumerate(cuts):
-        copies[12 + 2 * i].wait_recv()
-        copies[13 + 2 * i].wait_recv()
+        copies[14 + 2 * i].wait_recv()
+        copies[15 + 2 * i].wait_recv()
         multiply(
             2, i == 0, i == len(cuts) - 1, (opposite, start, size), (opposite, half + start, size)
         )
@@ -748,14 +775,13 @@
         in_specs=[pl.BlockSpec(memory_space=pl.ANY)] * 7,
         out_specs=(inner, inner),
         scratch_shapes=[
-            vmem((rows, depth), bf16),
+            vmem((rows + 3 * TAIL, depth), bf16),
             vmem(short_taps.shape, f32),
             table, table,
             vmem((1, width), f32),
             vmem((length, width), bf16),
             vmem((parts, depth, tile), bf16),
             vmem((3, rows, depth), bf16),
-            vmem((4 * TAIL, depth), bf16),
             vmem((3, parts, rows + 8, tile), f32),
             vmem((5, parts, 8, tile), f32),
             vmem((3, length + 8, width), f32),
@@ -779,7 +805,7 @@
             table, table,
             travelling, travelling,
             vmem((pieces, rows, depth // pieces), f32),
-            dma((6,)), dma((parts,)), dma((20,)), dma((20,)), dma((3,)), dma((3,)),
+            dma((6,)), dma((parts,)), dma((22,)), dma((22,)), dma((3,)), dma((3,)),
             dma((count,)), dma((count,)), dma((count,)), dma((count,)),
             dma((3, pieces)), dma((3, pieces)),
         ],

time: 91.4 us -> 91.4 us (level)
  no operation moved by 1% of the time
where the time goes in v3:
time: 91.4 us; the launch traced here: 91.2 us
  Pallas kernels  90.6 us (99%)
    pallas_call x1, Pallas kernels, square_shards(): pl.pallas_call(functools.partial(fused_kernel, count), out_shape=(pltpu.V...  89.4 us

profile of v3, /device:TPU:0, one launch (start us, length us, event | category | flops | bytes accessed | tf_op | source)
XLA Modules:
  0.0 91.2 jit_solution(15952932713019851085)
XLA Ops:
  0.6 89.4 %shard_map.86 = (bf16[512,512]{1,0:T(8,128)(2,1)S(1)}, bf16[128,4096]{1,0:T(8,128)(2,1)S(1)}) custom-call(bf16[128,4096]{1,0:T(8,128)(2,1)} %tok_hbm.1, bf16[3,4096,512]{2,1,0:T(8,128)(2,1)} %w_hbm.1, f32[3,3,512]{2,1,0:T(4,128)} %taps_hbm.1, f32[16,512]{1,0:T(8,128)} %rate_hbm.1, f32[16,512]{1,0:T(8,128)} %res_hbm.1, f32[1,512]{1,0:T(1,128)} %bitcast.1, ...), custom_call_target="tpu_custom_call" | custom-call | tf_op jit(solution)/shard_map/pallas_call | solution.py:769
  90.1 1.2 %shard_map.87 = (bf16[512,512]{1,0:T(8,128)(2,1)}, bf16[128,4096]{1,0:T(8,128)(2,1)}) custom-call(bf16[512,512]{1,0:T(8,128)(2,1)S(1)} %get-tuple-element.4.mixed, bf16[128,4096]{1,0:T(8,128)(2,1)S(1)} %get-tuple-element.5.grads), custom_call_target="tpu_custom_call" | custom-call | tf_op jit(solution)/shard_map/pallas_call | solution.py:741
